TPU v7x, 32 devices: a whole 2x2x4 slice. The times are simulated.
32 devices in a mesh: group: 4 (over z), expert: 4 (over y, x), replica: 2 (over core).
Axes of the slice: x: 2, y: 2, z: 4, core: 2. Of those that a mesh axis runs over, the one named last changes fastest.
Arguments:
- cotangent: bfloat16 [1024, 2048], P(('group', 'expert')), may hold values from -6 to 6
- expert_ids: int32 [2, 1024, 4], P('replica', ('group', 'expert')), may hold values from 0 to 7, all different within a row; in each aligned block of 64 rows (0 to 63, 64 to 127, ..., all dimensions but the last counted through in order) at most 64 rows name the same one
- gate_probs: float32 [2, 1024, 4], P('replica', ('group', 'expert')), may hold values from 0.05 to 1
- saved_gate: bfloat16 [16, 2048, 384], P(('group', 'expert'), 'replica'), may hold values from -6 to 6
- saved_up: bfloat16 [16, 2048, 384], P(('group', 'expert'), 'replica'), may hold values from -6 to 6
- w_gate: bfloat16 [16, 2048, 384], P(('group', 'expert')), may hold values from -0.21875 to 0.21875
- w_up: bfloat16 [16, 2048, 384], P(('group', 'expert')), may hold values from -0.21875 to 0.21875
- w_down: bfloat16 [16, 384, 2048], P(('group', 'expert')), may hold values from -0.21875 to 0.21875
Outputs:
- grad_input: bfloat16 [1024, 2048], P(('group', 'expert'), 'replica')
- grad_down: float32 [16, 384, 2048], P(('group', 'expert'), None, 'replica')
Inputs may be any that keep to these rules, and one draw needn't show every extreme that they name: `expert_ids`: each row of 4 entries names different experts. For each replica index and each block of 64 tokens no expert is named more than 64 times, and in every draw some expert is named exactly 64 times in some block.
All inputs are finite; a program needn't handle non-finite values.
Results may differ from a plain program's by a relative error of at most 0.0071.
Values may be sent and summed in bfloat16 or wider, within the bound.
A program may use at most 64 MiB of HBM per device.

v0:
```python
import jax
import jax.numpy as jnp
from jax import lax
from jax.sharding import PartitionSpec as P


def from_partner(value, axis, bit):
    mask = 2**bit
    pairs = [(source, source ^ mask) for source in range(lax.axis_size(axis))]
    return lax.ppermute(value, axis, pairs)


def on_device(cotangent, expert_ids, gate_probs, saved_gate, saved_up, w_gate, w_up, w_down):
    n_group = lax.axis_size("group")
    n_expert = lax.axis_size("expert")
    tok_rows, model_width = cotangent.shape
    pick_count = expert_ids.shape[2]
    experts = n_group * n_expert // 2
    half_width = model_width // 2
    capacity = saved_gate.shape[1] // (n_group * n_expert)
    assigned = tok_rows * pick_count
    flat_ids = expert_ids.reshape(assigned)
    positions = jnp.arange(assigned, dtype=jnp.int32)
    same_expert = (flat_ids[:, None] == flat_ids[None, :]) & (
        positions[None, :] < positions[:, None]
    )
    slot_pos = jnp.sum(same_expert.astype(jnp.int32), axis=1)
    target = flat_ids * capacity + slot_pos
    places = jnp.arange(experts * capacity, dtype=jnp.int32)
    dispatch_map = (places[:, None] == target[None, :]).astype(jnp.bfloat16)
    scaled = (gate_probs[0][:, :, None] * cotangent[:, None, :].astype(jnp.float32)).astype(
        jnp.bfloat16
    )
    scaled = scaled.reshape(assigned, model_width)
    packed = jnp.dot(dispatch_map, scaled, preferred_element_type=jnp.float32).astype(jnp.bfloat16)
    packed = packed.reshape(n_group // 2, n_expert, capacity, 2, half_width)
    packed = packed.transpose(0, 3, 1, 2, 4).reshape(n_group, n_expert, capacity, half_width)
    arrived = lax.all_to_all(
        lax.all_to_all(packed, "expert", split_axis=1, concat_axis=1, tiled=True),
        "group",
        split_axis=0,
        concat_axis=0,
        tiled=True,
    )
    partner = from_partner(arrived, "group", 0)
    low_half = lax.axis_index("group") % 2 == 0
    front_half = jnp.where(low_half, arrived, partner)
    back_half = jnp.where(low_half, partner, arrived)
    dy_slots = jnp.concatenate([front_half, back_half], axis=3).reshape(-1, model_width)
    pre_gate = saved_gate[0].astype(jnp.float32)
    pre_up = saved_up[0].astype(jnp.float32)
    sigmoid_gate = jax.nn.sigmoid(pre_gate)
    silu_gate = pre_gate * sigmoid_gate
    activation = (silu_gate * pre_up).astype(jnp.bfloat16)
    d_act = lax.dot_general(
        dy_slots, w_down[0], (((1,), (1,)), ((), ())), preferred_element_type=jnp.float32
    )
    d_gate = (d_act * pre_up * sigmoid_gate * (1.0 + pre_gate * (1.0 - sigmoid_gate))).astype(
        jnp.bfloat16
    )
    d_up = (d_act * silu_gate).astype(jnp.bfloat16)
    partial_value = lax.dot_general(
        d_gate, w_gate[0], (((1,), (1,)), ((), ())), preferred_element_type=jnp.float32
    )
    partial_value = partial_value + lax.dot_general(
        d_up, w_up[0], (((1,), (1,)), ((), ())), preferred_element_type=jnp.float32
    )
    partial_value = partial_value.astype(jnp.bfloat16)
    own_half = jnp.where(low_half, partial_value[:, :half_width], partial_value[:, half_width:])
    peer_half = jnp.where(low_half, partial_value[:, half_width:], partial_value[:, :half_width])
    received = from_partner(peer_half, "group", 0)
    combined = (own_half.astype(jnp.float32) + received.astype(jnp.float32)).astype(jnp.bfloat16)
    combined = combined.reshape(n_group, n_expert, capacity, half_width)
    grad_terms = lax.dot_general(
        activation, dy_slots, (((0,), (0,)), ((), ())), preferred_element_type=jnp.float32
    )
    returned = lax.all_to_all(
        lax.all_to_all(combined, "group", split_axis=0, concat_axis=0, tiled=True),
        "expert",
        split_axis=1,
        concat_axis=1,
        tiled=True,
    )
    home_rows = returned.reshape(n_group // 2, 2, n_expert, capacity, half_width)
    home_rows = home_rows.transpose(0, 2, 3, 1, 4).reshape(experts * capacity, model_width)
    per_assign = lax.dot_general(
        dispatch_map, home_rows, (((0,), (0,)), ((), ())), preferred_element_type=jnp.float32
    )
    home_sum = jnp.sum(per_assign.reshape(tok_rows, pick_count, model_width), axis=1)
    grad_down, grad_input = (
        lax.psum_scatter(grad_terms, "replica", scatter_dimension=1, tiled=True),
        lax.psum_scatter(home_sum, "replica", scatter_dimension=1, tiled=True),
    )
    return (grad_input.astype(jnp.bfloat16), grad_down[None])


def solution(mesh):
    return jax.shard_map(
        on_device,
        mesh=mesh,
        in_specs=(
            P(("group", "expert"), None),
            P("replica", ("group", "expert"), None),
            P("replica", ("group", "expert"), None),
            P(("group", "expert"), "replica", None),
            P(("group", "expert"), "replica", None),
            P(("group", "expert"), None, None),
            P(("group", "expert"), None, None),
            P(("group", "expert"), None, None),
        ),
        out_specs=(P(("group", "expert"), "replica"), P(("group", "expert"), None, "replica")),
        check_vma=False,
    )
```

profile of v0, /device:TPU:0, one launch (start us, length us, event | category | flops | bytes accessed | tf_op | source)
XLA Modules:
  0.0 327.0 jit_solution(2035328137108302808)
XLA Ops:
  7.2 0.0 copy-start
  7.2 0.9 copy.39
  8.1 0.1 reshape.73
  8.2 0.2 convert_reduce_fusion
  8.4 0.8 copy.40
  9.1 0.1 mul.55
  9.3 2.8 mul.57
  12.1 3.0 mul.58
  15.1 3.7 %convolution_convert_fusion = bf16[512,2048]{1,0:T(8,128)(2,1)} fusion(f32[256,2048]{1,0:T(8,128)} %mul.58, f32[256]{0:T(256)S(1)} %mul.55, s32[256]{0:T(256)S(1)} %multiply_add_fusion), kind=kOutput, calls=%fused_computation.3 | convolution fusion | flops 539099136 | bytes 4196352 | tf_op jit(solution)/shard_map/dot_general | solution.py:35
  18.8 4.5 %reshape.74 = bf16[2,4,64,2,1024]{4,3,2,1,0:T(2,128)(2,1)} reshape(bf16[512,2048]{1,0:T(8,128)(2,1)} %convolution_convert_fusion) | data formatting | bytes 4194304 | tf_op jit(solution)/shard_map/reshape | solution.py:36
  23.2 2.2 copy.47
  25.5 30.4 %all_to_all.20 = bf16[4,4,64,1024]{3,2,0,1:T(8,128)(2,1)S(1)} all-to-all(bf16[4,4,64,1024]{3,2,0,1:T(8,128)(2,1)S(1)} %bitcast.65), channel_id=1, replica_groups=mesh['group'=4,'expert'=4,'replica'=2] {'expert'}, dimensions={1} | all-to-all | bytes 4194304 | tf_op jit(solution)/shard_map/all_to_all | solution.py:39
  55.8 0.2 copy.43
  56.1 51.5 %all_to_all.21 = bf16[4,4,64,1024]{3,2,1,0:T(8,128)(2,1)} all-to-all(bf16[4,4,64,1024]{3,2,1,0:T(8,128)(2,1)S(1)} %copy.43), channel_id=1, replica_groups=mesh['group'=4,'expert'=4,'replica'=2] {'group'}, dimensions={0} | all-to-all | bytes 4194304 | tf_op jit(solution)/shard_map/all_to_all | solution.py:38
  107.6 0.2 collective-permute-start
  107.8 46.2 %collective-permute-done = bf16[4,4,64,1024]{3,2,1,0:T(8,128)(2,1)} collective-permute-done((bf16[4,4,64,1024]{3,2,1,0:T(8,128)(2,1)}, bf16[4,4,64,1024]{3,2,1,0:T(8,128)(2,1)}, u32[]{:S(2)}, u32[]{:S(2)}) %collective-permute-start) | collective-permute-done | bytes 2097184 | tf_op jit(solution)/shard_map/ppermute | solution.py:10
  153.9 2.5 broadcast_select_fusion.1
  156.4 0.0 copy-start.5
  156.4 0.4 pad_maximum_fusion
  156.9 0.0 copy-start.2
  156.9 1.9 copy-done.2
  158.8 0.0 copy-done.5
  158.8 2.3 fusion.20
  161.2 0.0 copy-start.3
  161.2 2.6 fusion.18
  163.8 2.4 add_convert_fusion
  166.2 0.2 broadcast_select_fusion.2
  166.4 0.4 collective-permute-start.1
  166.8 44.9 %collective-permute-done.1 = bf16[1024,1024]{1,0:T(8,128)(2,1)S(1)} collective-permute-done((bf16[1024,1024]{1,0:T(8,128)(2,1)S(1)}, bf16[1024,1024]{1,0:T(8,128)(2,1)S(1)}, u32[]{:S(2)}, u32[]{:S(2)}) %collective-permute-start.1) | collective-permute-done | bytes 2097184 | tf_op jit(solution)/shard_map/ppermute | solution.py:10
  211.7 1.5 add_convert_fusion.1
  213.2 48.5 %all_to_all.22 = bf16[4,4,64,1024]{3,2,1,0:T(8,128)(2,1)S(1)} all-to-all(bf16[4,4,64,1024]{3,2,1,0:T(8,128)(2,1)S(1)} %bitcast.67), channel_id=1, replica_groups=mesh['group'=4,'expert'=4,'replica'=2] {'group'}, dimensions={0} | all-to-all | bytes 4194304 | tf_op jit(solution)/shard_map/all_to_all | solution.py:78
  261.6 1.5 copy.44
  263.1 3.6 %all-to-all-start.3 = ((bf16[4,4,64,1024]{3,2,0,1:T(8,128)(2,1)}), bf16[4,4,64,1024]{3,2,0,1:T(8,128)(2,1)S(1)}, u32[]{:S(2)}, u32[]{:S(2)}) async-start(bf16[4,4,64,1024]{3,2,0,1:T(8,128)(2,1)} %copy.44), calls=%async_computation.3 | async-start | bytes 4194304 | tf_op jit(solution)/shard_map/all_to_all | solution.py:77
  266.7 0.2 reduce-scatter.3.cloned.1.call-start
  267.0 0.1 iota_compare_fusion.1
  267.1 0.1 eq.52
  267.2 22.7 %all-to-all-done.3 = bf16[4,4,64,1024]{3,2,0,1:T(8,128)(2,1)S(1)} async-done(((bf16[4,4,64,1024]{3,2,0,1:T(8,128)(2,1)}), bf16[4,4,64,1024]{3,2,0,1:T(8,128)(2,1)S(1)}, u32[]{:S(2)}, u32[]{:S(2)}) %all-to-all-start.3) | async-done | bytes 2097184 | tf_op jit(solution)/shard_map/all_to_all | solution.py:77
  289.9 3.5 %copy.51 = bf16[2,2,4,64,1024]{4,1,3,2,0:T(2,128)(2,1)} copy(bf16[2,2,4,64,1024]{4,3,1,0,2:T(8,128)(2,1)S(1)} %bitcast.64) | data formatting | bytes 4194304 | tf_op jit(solution)/shard_map/reshape | solution.py:84
  293.4 3.3 %reshape.82 = bf16[512,2048,1]{1,0,2:T(8,128)(2,1)S(1)} reshape(bf16[2,4,64,2,1024]{4,3,2,1,0:T(2,128)(2,1)} %bitcast.66) | data formatting | bytes 4194304 | tf_op jit(solution)/shard_map/reshape | solution.py:85
  296.7 1.5 convolution_reduce_fusion
  298.2 0.0 reduce-scatter.3.cloned.1.call-update
  298.2 0.0 reduce-scatter.5.cloned.1.call-start
  298.2 0.0 copy-start.1
  298.2 6.2 %fusion.25 = f32[384,2048]{1,0:T(8,128)} fusion(bf16[1024,2048]{1,0:T(8,128)(2,1)} %bitcast.69, bf16[1,1024,384]{2,1,0:T(8,128)(2,1)} %param.12, bf16[1,1024,384]{2,1,0:T(8,128)(2,1)S(1)} %copy-done.4), kind=kOutput, calls=%fused_computation.38 | convolution fusion | flops 1613758464 | bytes 8912896 | tf_op jit(solution)/shard_map/dot_general | solution.py:74
  304.4 0.0 reduce-scatter.5.cloned.1.call-update
  304.4 0.8 reduce-scatter.3.cloned.1.call-done
  305.2 1.6 convert_element_type.74
  306.8 13.3 %reduce-scatter.5.cloned.1.call-done = f32[384,1024]{1,0:T(8,128)} async-done(((f32[384,2048]{1,0:T(8,128)}), f32[384,1024]{1,0:T(8,128)}) %reduce-scatter.5.cloned.1.call-update) | async-done | bytes 1572880 | tf_op jit(solution)/shard_map/reduce_scatter | solution.py:91
  (8 shorter events, 0.0 us)
Async XLA Ops:
  7.2 154.0 %copy-start = (bf16[1,2048,384]{2,1,0:T(8,128)(2,1)S(1)}, bf16[1,2048,384]{2,1,0:T(8,128)(2,1)}, u32[]{:S(2)}) copy-start(bf16[1,2048,384]{2,1,0:T(8,128)(2,1)} %param.13) | copy-start | bytes 4718596
  107.6 46.4 %collective-permute-start = (bf16[4,4,64,1024]{3,2,1,0:T(8,128)(2,1)}, bf16[4,4,64,1024]{3,2,1,0:T(8,128)(2,1)}, u32[]{:S(2)}, u32[]{:S(2)}) collective-permute-start(bf16[4,4,64,1024]{3,2,1,0:T(8,128)(2,1)} %all_to_all.21), channel_id=1, source_target_pairs={{0,8},{8,0},{16,24},{24,16},{1,9},{9,1},{17,25},{25,17},{2,10},{10... | collective-permute-start | bytes 6291464 | tf_op jit(solution)/shard_map/ppermute | solution.py:10
  156.4 2.4 copy-start.5
  156.9 2.0 copy-start.2
  158.8 2.4 copy-start.4
  158.8 2.4 copy-start.6
  161.2 2.6 copy-start.3
  166.4 45.3 %collective-permute-start.1 = (bf16[1024,1024]{1,0:T(8,128)(2,1)S(1)}, bf16[1024,1024]{1,0:T(8,128)(2,1)S(1)}, u32[]{:S(2)}, u32[]{:S(2)}) collective-permute-start(bf16[1024,1024]{1,0:T(8,128)(2,1)S(1)} %broadcast_select_fusion.2), channel_id=1, source_target_pairs={{0,8},{8,0},{16,24},{24,16},{1,9},{9,1},{17,25},{25,17},{2,10},{10... | collective-permute-start | bytes 6291464 | tf_op jit(solution)/shard_map/ppermute | solution.py:10
  263.1 26.8 %all-to-all-start.3 = ((bf16[4,4,64,1024]{3,2,0,1:T(8,128)(2,1)}), bf16[4,4,64,1024]{3,2,0,1:T(8,128)(2,1)S(1)}, u32[]{:S(2)}, u32[]{:S(2)}) async-start(bf16[4,4,64,1024]{3,2,0,1:T(8,128)(2,1)} %copy.44), calls=%async_computation.3 | async-start | bytes 4194304 | tf_op jit(solution)/shard_map/all_to_all | solution.py:77
  266.7 38.5 %reduce-scatter.3.cloned.1.call-start = ((), (), s32[]{:S(2)}) async-start(), calls=%async_computation.6 | async-start | bytes 786432 | tf_op jit(solution)/shard_map/reduce_scatter | solution.py:92
  298.2 22.0 %reduce-scatter.5.cloned.1.call-start = ((), (), s32[]{:S(2)}) async-start(), calls=%async_computation.7 | async-start | bytes 4718592 | tf_op jit(solution)/shard_map/reduce_scatter | solution.py:91
  298.2 21.9 %copy-start.1 = (bf16[1,2048,384]{2,1,0:T(8,128)(2,1)S(1)}, bf16[1,2048,384]{2,1,0:T(8,128)(2,1)}, u32[]{:S(2)}) copy-start(bf16[1,2048,384]{2,1,0:T(8,128)(2,1)} %param.13) | copy-start | bytes 4718596
Sparse Core Ops, SparseCore 0:
  298.3 6.8 reduce-scatter.2
  308.0 12.0 reduce-scatter.4
where the time goes:
time: 328 us; the launch traced here: 327 us
  blocking collectives  130 us (40%)
  waiting for transfers between devices  128 us (39%)
  local copies, waits for them, and re-layouts  24.9 us (8%)
  matrix products  18.7 us (6%)
  between operations  14.2 us (4%)
  other arithmetic  6.58 us (2%)
  starting transfers between devices  4.44 us (1%)
    ppermute x2, waiting for transfers between devices, from_partner(): return lax.ppermute(value, axis, pairs)  91.1 us
    all_to_all x1, blocking collectives, on_device(): lax.all_to_all(lax.all_to_all(packed, 'expert', split_axis=1, concat_axis...  51.5 us
    all_to_all x1, blocking collectives, on_device(): lax.all_to_all(combined, 'group', split_axis=0, concat_axis=0, tiled=True)  48.5 us
    all_to_all x1, blocking collectives, on_device(): lax.all_to_all(packed, 'expert', split_axis=1, concat_axis=1, tiled=True)  30.4 us
    all_to_all x1, waiting for transfers between devices, on_device(): lax.all_to_all(lax.all_to_all(combined, 'group', split_axis=0, concat_axi...  22.7 us
    reduce_scatter x1, waiting for transfers between devices, on_device(): lax.psum_scatter(grad_terms, 'replica', scatter_dimension=1, tiled=True)  13.3 us
  transfers between devices with their start and end apart: 5, of which 5 were waited for; matrix products, arithmetic and copies ran while one was open for 2% of the time, Pallas kernels for 0%

commit v1 on v0

--- a/solution.py
+++ b/solution.py
@@ -1,7 +1,14 @@
+import functools
+
 import jax
 import jax.numpy as jnp
 from jax import lax
+from jax.experimental import pallas as pl
+from jax.experimental.pallas import tpu as pltpu
 from jax.sharding import PartitionSpec as P
+
+MESH = pl.DeviceIdType.MESH
+NT = (((1,), (1,)), ((), ()))
 
 
 def from_partner(value, axis, bit):
@@ -10,7 +17,7 @@
     return lax.ppermute(value, axis, pairs)
 
 
-def on_device(cotangent, expert_ids, gate_probs, saved_gate, saved_up, w_gate, w_up, w_down):
+def routed_plan(cotangent, expert_ids, gate_probs, saved_gate, saved_up, w_gate, w_up, w_down):
     n_group = lax.axis_size("group")
     n_expert = lax.axis_size("expert")
     tok_rows, model_width = cotangent.shape
@@ -92,6 +99,420 @@
         lax.psum_scatter(home_sum, "replica", scatter_dimension=1, tiled=True),
     )
     return (grad_input.astype(jnp.bfloat16), grad_down[None])
+
+
+def dense_kernel(
+    n_group,
+    n_expert,
+    cot_ref,
+    ids_ref,
+    prob_ref,
+    sg_ref,
+    su_ref,
+    wg_ref,
+    wu_ref,
+    wd_ref,
+    out_ref,
+    gd_ref,
+    cot_all,
+    meta_all,
+    act_t,
+    f_gate,
+    f_up,
+    own_buf,
+    sib_send,
+    sib_recv,
+    p_buf,
+    ra,
+    rb,
+    a2,
+    b2,
+    ra2,
+    rb2,
+    z_send,
+    z_recv,
+    gt_send,
+    gt_recv,
+    ssem,
+    rsem,
+    gsem,
+    lsem,
+):
+    tok, width = cot_ref.shape
+    half = width // 2
+    quarter = half // 2
+    rows_g = n_expert * tok
+    picks = ids_ref.shape[1]
+    experts = meta_all.shape[1]
+    f32, bf16 = jnp.float32, jnp.bfloat16
+    g = lax.axis_index("group")
+    ex = lax.axis_index("expert")
+    r = lax.axis_index("replica")
+    x, y = ex % 2, ex // 2
+    nx, ny = 1 - x, 1 - y
+    ex_x, ex_y, ex_d = y * 2 + nx, ny * 2 + x, ny * 2 + nx
+    x_dev, y_dev, d_dev = (g, ex_x, r), (g, ex_y, r), (g, ex_d, r)
+    sib_dev = (g, ex, 1 - r)
+
+    def group_at(i):
+        low = (g % 2 + i % 2) % 2
+        high = (g // 2 + i // 2) % 2
+        return low + 2 * high
+
+    my_col = pl.multiple_of(r * half, half)
+    sib_col = pl.multiple_of((1 - r) * half, half)
+    col_a = my_col
+    col_b = pl.multiple_of(r * half + quarter, quarter)
+
+    def row_of(q, e):
+        return pl.multiple_of((q * n_expert + e) * tok, tok)
+
+    def rcopy(kind, i, src, dst, dev):
+        return pltpu.make_async_remote_copy(
+            src_ref=src,
+            dst_ref=dst,
+            send_sem=ssem.at[kind, i],
+            recv_sem=rsem.at[kind, i],
+            device_id=dev,
+            device_id_type=MESH,
+        )
+
+    def block(q, e, col, size):
+        return cot_all.at[pl.ds(row_of(q, e), tok), pl.ds(col, size)]
+
+    def z_dev(i):
+        return (group_at(i), ex, r)
+
+    def ag_z(i, recv):
+        land = block(group_at(i), ex, my_col, half) if recv else block(g, ex, my_col, half)
+        src = land if recv else cot_ref.at[:, pl.ds(my_col, half)]
+        return rcopy(0, i, src, land, z_dev(i))
+
+    def ag_mz(i, recv):
+        ref = meta_all.at[(group_at(i) if recv else g) * n_expert + ex]
+        return rcopy(1, i, ref, ref, z_dev(i))
+
+    def ag_xy(kind, i, e, col, dev):
+        ref = block(group_at(i), e, col, quarter)
+        return rcopy(kind, i, ref, ref, dev)
+
+    def ag_meta(kind, i, e, dev):
+        ref = meta_all.at[group_at(i) * n_expert + e]
+        return rcopy(kind, i, ref, ref, dev)
+
+    def ag_sib(i, recv):
+        rows = pl.ds(row_of(group_at(i), 0), rows_g)
+        ref = cot_all.at[rows, pl.ds(sib_col if recv else my_col, half)]
+        return rcopy(11, i, ref, ref, sib_dev)
+
+    def rs_sib(i):
+        return rcopy(12, i, sib_send.at[i], sib_recv.at[i], sib_dev)
+
+    def rs_a1(i):
+        return rcopy(13, i, p_buf.at[i, ny, :, :, pl.ds(0, quarter)], ra.at[i], y_dev)
+
+    def rs_b1(i):
+        return rcopy(14, i, p_buf.at[i, :, nx, :, pl.ds(quarter, quarter)], rb.at[i], x_dev)
+
+    def rs_a2(i):
+        return rcopy(15, i, a2.at[i, nx], ra2.at[i], x_dev)
+
+    def rs_b2(i):
+        return rcopy(16, i, b2.at[i, ny], rb2.at[i], y_dev)
+
+    def rs_z(i):
+        return rcopy(17, i, z_send.at[i], z_recv.at[i], z_dev(i))
+
+    grad_copy = pltpu.make_async_remote_copy(
+        src_ref=gt_send,
+        dst_ref=gt_recv,
+        send_sem=gsem.at[0],
+        recv_sem=gsem.at[1],
+        device_id=sib_dev,
+        device_id_type=MESH,
+    )
+
+    barrier = pltpu.get_barrier_semaphore()
+    peers = [z_dev(i) for i in range(1, n_group)] + [x_dev, y_dev, d_dev, sib_dev]
+    for dev in peers:
+        pl.semaphore_signal(barrier, inc=1, device_id=dev, device_id_type=MESH)
+
+    place = pltpu.make_async_copy(
+        cot_ref.at[:, pl.ds(my_col, half)], block(g, ex, my_col, half), lsem
+    )
+    place.start()
+    lane = lax.broadcasted_iota(jnp.int32, (tok, 128), 1)
+    named = jnp.zeros((tok, 128), f32)
+    weight = jnp.zeros((tok, 128), f32)
+    for k in range(picks):
+        same = ids_ref[:, k : k + 1] == lane
+        named = named + jnp.where(same, 1.0, 0.0)
+        weight = weight + jnp.where(same, prob_ref[:, k : k + 1], 0.0)
+    before = lax.broadcasted_iota(jnp.int32, (tok, tok), 0) > lax.broadcasted_iota(
+        jnp.int32, (tok, tok), 1
+    )
+    slot = jnp.dot(
+        jnp.where(before, 1.0, 0.0).astype(bf16), named.astype(bf16), preferred_element_type=f32
+    )
+    slot = jnp.where(named > 0.5, slot, -1.0)
+    meta_all[g * n_expert + ex] = jnp.concatenate([slot, weight], axis=0).T[:experts]
+    place.wait()
+    pl.semaphore_wait(barrier, len(peers))
+
+    for i in range(1, n_group):
+        ag_mz(i, False).start()
+    for i in range(1, n_group):
+        ag_z(i, False).start()
+
+    expert = (g // 2) * n_expert + ex
+    eye = lax.broadcasted_iota(jnp.int32, (2 * tok, 2 * tok), 0) == lax.broadcasted_iota(
+        jnp.int32, (2 * tok, 2 * tok), 1
+    )
+    place_lane = lax.broadcasted_iota(jnp.int32, (tok, rows_g), 1).astype(f32)
+
+    def ag_first(i):
+        @pl.when(i > 0)
+        def _():
+            ag_mz(i, True).wait_recv()
+            ag_z(i, True).wait_recv()
+
+        ag_meta(8, i, ex, x_dev).start()
+        ag_meta(9, i, ex, y_dev).start()
+        ag_meta(10, i, ex, d_dev).start()
+        ag_xy(2, i, ex, col_a, x_dev).start()
+        ag_xy(3, i, ex, col_b, y_dev).start()
+        ag_xy(4, i, ex, col_b, x_dev).start()
+        ag_xy(5, i, ex, col_a, y_dev).start()
+
+    def ag_second(i):
+        ag_xy(2, i, ex_x, col_a, x_dev).wait_recv()
+        ag_xy(6, i, ex_x, col_a, y_dev).start()
+        ag_xy(3, i, ex_y, col_b, y_dev).wait_recv()
+        ag_xy(7, i, ex_y, col_b, x_dev).start()
+
+    def ag_third(i):
+        q = group_at(i)
+        ag_meta(8, i, ex_x, x_dev).wait_recv()
+        ag_meta(9, i, ex_y, y_dev).wait_recv()
+        ag_meta(10, i, ex_d, d_dev).wait_recv()
+        picked, weights = [], []
+        for b in range(n_expert):
+            row = meta_all[q * n_expert + b, pl.ds(expert, 1), :]
+            col = jnp.sum(jnp.where(eye, row, 0.0), axis=1, keepdims=True)
+            slot_col = col[:tok]
+            target = jnp.where(slot_col < -0.5, -1.0, slot_col + float(b * tok))
+            picked.append(jnp.where(place_lane == target, 1.0, 0.0))
+            weights.append(col[tok:])
+        select = jnp.concatenate(picked, axis=0).astype(bf16)
+        weights = jnp.concatenate(weights, axis=0)
+        rows = pl.ds(pl.multiple_of(q * rows_g, rows_g), rows_g)
+        gate = jnp.dot(select, sg_ref[0, rows, :], preferred_element_type=f32)
+        up = jnp.dot(select, su_ref[0, rows, :], preferred_element_type=f32)
+        sig = jax.nn.sigmoid(gate)
+        silu = gate * sig
+        act_t[:, rows] = (silu * up * weights).T.astype(bf16)
+        f_gate[i] = weights * up * sig * (1.0 + gate * (1.0 - sig))
+        f_up[i] = weights * silu
+        ag_xy(4, i, ex_x, col_b, x_dev).wait_recv()
+        ag_xy(5, i, ex_y, col_a, y_dev).wait_recv()
+        ag_xy(6, i, ex_d, col_a, y_dev).wait_recv()
+        ag_xy(7, i, ex_d, col_b, x_dev).wait_recv()
+        ag_sib(i, False).start()
+
+    def compute(i):
+        q = group_at(i)
+        ag_sib(i, True).wait_recv()
+        rows = pl.ds(pl.multiple_of(q * rows_g, rows_g), rows_g)
+        d_act = lax.dot_general(
+            cot_all[rows, :], wd_ref[0], NT, preferred_element_type=f32
+        )
+        d_gate = (d_act * f_gate[i]).astype(bf16)
+        d_up = (d_act * f_up[i]).astype(bf16)
+
+        def partial_of(col):
+            wide = pl.ds(col, half)
+            value = lax.dot_general(d_gate, wg_ref[0, wide, :], NT, preferred_element_type=f32)
+            return value + lax.dot_general(
+                d_up, wu_ref[0, wide, :], NT, preferred_element_type=f32
+            )
+
+        sib_send[i] = partial_of(sib_col).astype(bf16)
+        rs_sib(i).start()
+        own_buf[i] = partial_of(my_col).astype(bf16)
+
+    def rs_first(i):
+        rs_sib(i).wait_recv()
+        total = own_buf[i].astype(f32) + sib_recv[i].astype(f32)
+        p_buf[i] = total.astype(bf16).reshape(2, 2, tok, half)
+        rs_a1(i).start()
+        rs_b1(i).start()
+
+    def rs_second(i):
+        rs_a1(i).wait_recv()
+        left = p_buf[i, y, :, :, pl.ds(0, quarter)].astype(f32) + ra[i].astype(f32)
+        a2[i] = left.astype(bf16)
+        rs_a2(i).start()
+        rs_b1(i).wait_recv()
+        right = p_buf[i, :, x, :, pl.ds(quarter, quarter)].astype(f32) + rb[i].astype(f32)
+        b2[i] = right.astype(bf16)
+        rs_b2(i).start()
+
+    def rs_third(i):
+        rs_a2(i).wait_recv()
+        rs_b2(i).wait_recv()
+        left = a2[i, x].astype(f32) + ra2[i].astype(f32)
+        right = b2[i, y].astype(f32) + rb2[i].astype(f32)
+        z_send[i] = jnp.concatenate([left, right], axis=1).astype(bf16)
+
+        @pl.when(i > 0)
+        def _():
+            rs_z(i).start()
+
+    def grad_chunk(j):
+        base = jnp.where(j < 2, 1 - r, r) * half + (j % 2) * quarter
+        cols = pl.ds(pl.multiple_of(base, quarter), quarter)
+        value = jnp.dot(act_t[...], cot_all[:, cols], preferred_element_type=f32)
+        land = pl.ds(pl.multiple_of((j % 2) * quarter, quarter), quarter)
+
+        @pl.when(j < 2)
+        def _():
+            gt_send[:, land] = value.astype(bf16)
+
+        @pl.when(j >= 2)
+        def _():
+            gd_ref[0, :, land] = value
+
+        @pl.when(j == 1)
+        def _():
+            grad_copy.start()
+
+    stages = (ag_first, ag_second, ag_third, compute, rs_first, rs_second, rs_third)
+    order = (0, 1, 4, 5, 6, 2, 3)
+    last = n_group + len(stages) - 1
+
+    def step(s, carry):
+        for lag in order:
+
+            @pl.when((s >= lag) & (s < lag + n_group))
+            def _(lag=lag):
+                stages[lag](s - lag)
+
+        @pl.when(s >= last - 4)
+        def _():
+            grad_chunk(s - (last - 4))
+
+        return carry
+
+    lax.fori_loop(0, last, step, 0)
+
+    grad_copy.wait_recv()
+    gd_ref[0] = gd_ref[0] + gt_recv[...].astype(f32)
+    total = z_send[0].astype(f32)
+    for i in range(1, n_group):
+        rs_z(i).wait_recv()
+        total = total + z_recv[i].astype(f32)
+    out_ref[...] = total.astype(bf16)
+
+    grad_copy.wait_send()
+
+    def drain(i, carry):
+        @pl.when(i > 0)
+        def _():
+            ag_z(i, False).wait_send()
+            ag_mz(i, False).wait_send()
+            rs_z(i).wait_send()
+
+        ag_meta(8, i, ex, x_dev).wait_send()
+        ag_meta(9, i, ex, y_dev).wait_send()
+        ag_meta(10, i, ex, d_dev).wait_send()
+        ag_xy(2, i, ex, col_a, x_dev).wait_send()
+        ag_xy(3, i, ex, col_b, y_dev).wait_send()
+        ag_xy(4, i, ex, col_b, x_dev).wait_send()
+        ag_xy(5, i, ex, col_a, y_dev).wait_send()
+        ag_xy(6, i, ex_x, col_a, y_dev).wait_send()
+        ag_xy(7, i, ex_y, col_b, x_dev).wait_send()
+        ag_sib(i, False).wait_send()
+        rs_sib(i).wait_send()
+        rs_a1(i).wait_send()
+        rs_b1(i).wait_send()
+        rs_a2(i).wait_send()
+        rs_b2(i).wait_send()
+        return carry
+
+    lax.fori_loop(0, n_group, drain, 0)
+
+
+def dense_plan(cotangent, expert_ids, gate_probs, saved_gate, saved_up, w_gate, w_up, w_down):
+    n_group = lax.axis_size("group")
+    n_expert = lax.axis_size("expert")
+    tok, width = cotangent.shape
+    half, quarter = width // 2, width // 4
+    hidden = w_down.shape[1]
+    experts = n_group * n_expert // 2
+    blocks = n_group * n_expert
+    rows_g = n_expert * tok
+    bf16, f32 = jnp.bfloat16, jnp.float32
+    vmem = pl.BlockSpec(memory_space=pltpu.VMEM)
+    kinds = 18
+    return pl.pallas_call(
+        functools.partial(dense_kernel, n_group, n_expert),
+        out_shape=(
+            jax.ShapeDtypeStruct((tok, half), bf16),
+            jax.ShapeDtypeStruct((1, hidden, half), f32),
+        ),
+        in_specs=[vmem] * 8,
+        out_specs=(vmem, vmem),
+        scratch_shapes=[
+            pltpu.VMEM((blocks * tok, width), bf16),
+            pltpu.VMEM((blocks, experts, 2 * tok), f32),
+            pltpu.VMEM((hidden, blocks * tok), bf16),
+            pltpu.VMEM((n_group, rows_g, hidden), f32),
+            pltpu.VMEM((n_group, rows_g, hidden), f32),
+            pltpu.VMEM((n_group, rows_g, half), bf16),
+            pltpu.VMEM((n_group, rows_g, half), bf16),
+            pltpu.VMEM((n_group, rows_g, half), bf16),
+            pltpu.VMEM((n_group, 2, 2, tok, half), bf16),
+            pltpu.VMEM((n_group, 2, tok, quarter), bf16),
+            pltpu.VMEM((n_group, 2, tok, quarter), bf16),
+            pltpu.VMEM((n_group, 2, tok, quarter), bf16),
+            pltpu.VMEM((n_group, 2, tok, quarter), bf16),
+            pltpu.VMEM((n_group, tok, quarter), bf16),
+            pltpu.VMEM((n_group, tok, quarter), bf16),
+            pltpu.VMEM((n_group, tok, half), bf16),
+            pltpu.VMEM((n_group, tok, half), bf16),
+            pltpu.VMEM((hidden, half), bf16),
+            pltpu.VMEM((hidden, half), bf16),
+            pltpu.SemaphoreType.DMA((kinds, n_group)),
+            pltpu.SemaphoreType.DMA((kinds, n_group)),
+            pltpu.SemaphoreType.DMA((2,)),
+            pltpu.SemaphoreType.DMA,
+        ],
+        compiler_params=pltpu.CompilerParams(
+            collective_id=0, has_side_effects=True, vmem_limit_bytes=60 * 1024 * 1024
+        ),
+    )(
+        cotangent,
+        expert_ids[0],
+        gate_probs[0],
+        saved_gate,
+        saved_up,
+        w_gate,
+        w_up,
+        w_down,
+    )
+
+
+def on_device(cotangent, expert_ids, gate_probs, saved_gate, saved_up, w_gate, w_up, w_down):
+    n_group = lax.axis_size("group")
+    n_expert = lax.axis_size("expert")
+    n_replica = lax.axis_size("replica")
+    tok_rows = cotangent.shape[0]
+    capacity = saved_gate.shape[1] // (n_group * n_expert)
+    small = n_group == 4 and n_expert == 4 and n_replica == 2
+    plan = routed_plan
+    if small and capacity == tok_rows and 2 * tok_rows == 128:
+        plan = dense_plan
+    return plan(cotangent, expert_ids, gate_probs, saved_gate, saved_up, w_gate, w_up, w_down)
 
 
 def solution(mesh):

time: 328 us -> 68.9 us (0.21)
  blocking collectives: 130 us -> 0 us
  waiting for transfers between devices: 128 us -> 0 us
  Pallas kernels: 0 us -> 60.4 us
  matrix products: 18.7 us -> 0 us
  local copies, waits for them, and re-layouts: 24.9 us -> 7.06 us
  between operations: 14.2 us -> 0.64 us
  other arithmetic: 6.58 us -> 0 us
  starting transfers between devices: 4.44 us -> 0 us
    all_to_all x3 -> x0, blocking collectives: 130 us -> none  [the longest x1 51.5 us: on_device(): lax.all_to_all(lax.all_to_all(packed, 'expert', split_axis=1, concat_axis...]
    ppermute x2 -> x0, waiting for transfers between devices: 91.1 us -> none  [from_partner(): return lax.ppermute(value, axis, pairs)]
    pallas_call x0 -> x1, Pallas kernels: none -> 60.4 us  [dense_plan(): pl.pallas_call(functools.partial(dense_kernel, n_group, n_expert), out_sh...]
    all_to_all x1 -> x0, waiting for transfers between devices: 22.7 us -> none  [on_device(): lax.all_to_all(lax.all_to_all(combined, 'group', split_axis=0, concat_axi...]
    dot_general x6 -> x0, matrix products: 18.7 us -> none  [the longest x1 6.16 us: on_device(): lax.dot_general(activation, dy_slots, (((0,), (0,)), ((), ())), preferred...]
    reduce_scatter x2 -> x0, waiting for transfers between devices: 14.1 us -> none  [the longest x1 13.3 us: on_device(): lax.psum_scatter(grad_terms, 'replica', scatter_dimension=1, tiled=True)]
    reshape x5 -> x0, local copies, waits for them, and re-layouts: 13.6 us -> none  [the longest x1 4.48 us: on_device(): packed = packed.reshape(n_group // 2, n_expert, capacity, 2, half_width)]
    mul x3 -> x0, local copies, waits for them, and re-layouts: 5.91 us -> none  [on_device(): gate_probs[0][:, :, None] * cotangent[:, None, :].astype(jnp.float32)]
  transfers between devices with their start and end apart: 5 -> 0, of which waited for: 5 -> 0; matrix products, arithmetic and copies ran while one was open for 2% -> 0% of each run, Pallas kernels for 0% -> 0%
where the time goes in v1:
time: 68.9 us; the launch traced here: 68.1 us
  Pallas kernels  60.4 us (88%)
  local copies, waits for them, and re-layouts  7.06 us (10%)
    pallas_call x1, Pallas kernels, dense_plan(): pl.pallas_call(functools.partial(dense_kernel, n_group, n_expert), out_sh...  60.4 us
    unnamed x4, local copies, waits for them, and re-layouts  7.06 us

profile of v1, /device:TPU:0, one launch (start us, length us, event | category | flops | bytes accessed | tf_op | source)
XLA Modules:
  0.0 68.1 jit_solution(5550798010523578239)
XLA Ops:
  0.6 1.4 %copy.10 = s32[1,64,4]{2,1,0:T(8,128)} copy(s32[1,64,4]{1,2,0:T(4,128)} %param.9) | data formatting | bytes 2048 | tf_op args[1]
  2.0 1.4 %copy.11 = f32[1,64,4]{2,1,0:T(8,128)} copy(f32[1,64,4]{1,2,0:T(4,128)} %param.10) | data formatting | bytes 2048 | tf_op args[2]
  3.4 60.4 %shard_map.95 = (bf16[64,1024]{1,0:T(8,128)(2,1)}, f32[1,384,1024]{2,1,0:T(8,128)}) custom-call(bf16[64,2048]{1,0:T(8,128)(2,1)} %cot_ref.1, s32[64,4]{1,0:T(8,128)} %bitcast.2, f32[64,4]{1,0:T(8,128)} %bitcast.3, bf16[1,1024,384]{2,1,0:T(8,128)(2,1)} %sg_ref.1, bf16[1,1024,384]{2,1,0:T(8,128)(2,1)} %su_ref.1, bf16[1,2048,384]{2,1,0:T(8,128)(2,1)} %wg_ref.1, ...), custom_call_target="tpu_custom_call" | custom-call | tf_op jit(solution)/shard_map/pallas_call | solution.py:457
  63.8 1.6 %copy.14 = bf16[64,1024]{1,0:T(8,128)(2,1)} copy(bf16[64,1024]{1,0:T(8,128)(2,1)} %get-tuple-element.4) | data formatting | bytes 262144
  65.3 2.7 %copy.15 = f32[1,384,1024]{2,1,0:T(8,128)} copy(f32[1,384,1024]{2,1,0:T(8,128)} %get-tuple-element.5) | data formatting | bytes 3145728

commit v2 on v1

--- a/solution.py
+++ b/solution.py
@@ -107,13 +107,19 @@
     cot_ref,
     ids_ref,
     prob_ref,
+    sg_hbm,
+    su_hbm,
+    wg_hbm,
+    wu_hbm,
+    wd_hbm,
+    out_ref,
+    gd_ref,
+    gt_recv,
     sg_ref,
     su_ref,
     wg_ref,
     wu_ref,
     wd_ref,
-    out_ref,
-    gd_ref,
     cot_all,
     meta_all,
     act_t,
@@ -132,7 +138,6 @@
     z_send,
     z_recv,
     gt_send,
-    gt_recv,
     ssem,
     rsem,
     gsem,
@@ -142,7 +147,7 @@
     half = width // 2
     quarter = half // 2
     rows_g = n_expert * tok
-    picks = ids_ref.shape[1]
+    picks = ids_ref.shape[0]
     experts = meta_all.shape[1]
     f32, bf16 = jnp.float32, jnp.bfloat16
     g = lax.axis_index("group")
@@ -185,8 +190,7 @@
 
     def ag_z(i, recv):
         land = block(group_at(i), ex, my_col, half) if recv else block(g, ex, my_col, half)
-        src = land if recv else cot_ref.at[:, pl.ds(my_col, half)]
-        return rcopy(0, i, src, land, z_dev(i))
+        return rcopy(0, i, land, land, z_dev(i))
 
     def ag_mz(i, recv):
         ref = meta_all.at[(group_at(i) if recv else g) * n_expert + ex]
@@ -238,24 +242,38 @@
         pl.semaphore_signal(barrier, inc=1, device_id=dev, device_id_type=MESH)
 
     place = pltpu.make_async_copy(
-        cot_ref.at[:, pl.ds(my_col, half)], block(g, ex, my_col, half), lsem
+        cot_ref.at[:, pl.ds(my_col, half)], block(g, ex, my_col, half), lsem.at[0]
     )
     place.start()
-    lane = lax.broadcasted_iota(jnp.int32, (tok, 128), 1)
-    named = jnp.zeros((tok, 128), f32)
-    weight = jnp.zeros((tok, 128), f32)
+    loads = [
+        pltpu.make_async_copy(src, dst, lsem.at[1 + k])
+        for k, (src, dst) in enumerate(
+            [
+                (sg_hbm, sg_ref),
+                (su_hbm, su_ref),
+                (wd_hbm, wd_ref),
+                (wg_hbm, wg_ref),
+                (wu_hbm, wu_ref),
+            ]
+        )
+    ]
+    for load in loads:
+        load.start()
+    named_by = lax.broadcasted_iota(jnp.int32, (experts, tok), 0)
+    named = jnp.zeros((experts, tok), f32)
+    weight = jnp.zeros((experts, tok), f32)
     for k in range(picks):
-        same = ids_ref[:, k : k + 1] == lane
+        same = ids_ref[k : k + 1, :] == named_by
         named = named + jnp.where(same, 1.0, 0.0)
-        weight = weight + jnp.where(same, prob_ref[:, k : k + 1], 0.0)
-    before = lax.broadcasted_iota(jnp.int32, (tok, tok), 0) > lax.broadcasted_iota(
+        weight = weight + jnp.where(same, prob_ref[k : k + 1, :], 0.0)
+    before = lax.broadcasted_iota(jnp.int32, (tok, tok), 0) < lax.broadcasted_iota(
         jnp.int32, (tok, tok), 1
     )
     slot = jnp.dot(
-        jnp.where(before, 1.0, 0.0).astype(bf16), named.astype(bf16), preferred_element_type=f32
+        named.astype(bf16), jnp.where(before, 1.0, 0.0).astype(bf16), preferred_element_type=f32
     )
     slot = jnp.where(named > 0.5, slot, -1.0)
-    meta_all[g * n_expert + ex] = jnp.concatenate([slot, weight], axis=0).T[:experts]
+    meta_all[g * n_expert + ex] = jnp.concatenate([slot, weight], axis=1)
     place.wait()
     pl.semaphore_wait(barrier, len(peers))
 
@@ -306,6 +324,12 @@
         select = jnp.concatenate(picked, axis=0).astype(bf16)
         weights = jnp.concatenate(weights, axis=0)
         rows = pl.ds(pl.multiple_of(q * rows_g, rows_g), rows_g)
+
+        @pl.when(i == 0)
+        def _():
+            for load in loads[:2]:
+                load.wait()
+
         gate = jnp.dot(select, sg_ref[0, rows, :], preferred_element_type=f32)
         up = jnp.dot(select, su_ref[0, rows, :], preferred_element_type=f32)
         sig = jax.nn.sigmoid(gate)
@@ -321,6 +345,12 @@
 
     def compute(i):
         q = group_at(i)
+
+        @pl.when(i == 0)
+        def _():
+            for load in loads[2:]:
+                load.wait()
+
         ag_sib(i, True).wait_recv()
         rows = pl.ds(pl.multiple_of(q * rows_g, rows_g), rows_g)
         d_act = lax.dot_general(
@@ -338,11 +368,11 @@
 
         sib_send[i] = partial_of(sib_col).astype(bf16)
         rs_sib(i).start()
-        own_buf[i] = partial_of(my_col).astype(bf16)
+        own_buf[i] = partial_of(my_col)
 
     def rs_first(i):
         rs_sib(i).wait_recv()
-        total = own_buf[i].astype(f32) + sib_recv[i].astype(f32)
+        total = own_buf[i] + sib_recv[i].astype(f32)
         p_buf[i] = total.astype(bf16).reshape(2, 2, tok, half)
         rs_a1(i).start()
         rs_b1(i).start()
@@ -380,7 +410,7 @@
 
         @pl.when(j >= 2)
         def _():
-            gd_ref[0, :, land] = value
+            gd_ref[:, land] = value
 
         @pl.when(j == 1)
         def _():
@@ -406,7 +436,6 @@
     lax.fori_loop(0, last, step, 0)
 
     grad_copy.wait_recv()
-    gd_ref[0] = gd_ref[0] + gt_recv[...].astype(f32)
     total = z_send[0].astype(f32)
     for i in range(1, n_group):
         rs_z(i).wait_recv()
@@ -442,6 +471,11 @@
     lax.fori_loop(0, n_group, drain, 0)
 
 
+def finish_kernel(rows_ref, own_ref, other_ref, out_ref, gd_ref):
+    out_ref[...] = rows_ref[...]
+    gd_ref[0] = own_ref[...] + other_ref[...].astype(jnp.float32)
+
+
 def dense_plan(cotangent, expert_ids, gate_probs, saved_gate, saved_up, w_gate, w_up, w_down):
     n_group = lax.axis_size("group")
     n_expert = lax.axis_size("expert")
@@ -454,21 +488,32 @@
     bf16, f32 = jnp.bfloat16, jnp.float32
     vmem = pl.BlockSpec(memory_space=pltpu.VMEM)
     kinds = 18
-    return pl.pallas_call(
+    cotangent, saved_gate, saved_up, w_gate, w_up, w_down = (
+        pltpu.with_memory_space_constraint(value, pltpu.HBM)
+        for value in (cotangent, saved_gate, saved_up, w_gate, w_up, w_down)
+    )
+    here = pl.BlockSpec(memory_space=pltpu.HBM)
+    rows, own, other = pl.pallas_call(
         functools.partial(dense_kernel, n_group, n_expert),
         out_shape=(
             jax.ShapeDtypeStruct((tok, half), bf16),
-            jax.ShapeDtypeStruct((1, hidden, half), f32),
+            jax.ShapeDtypeStruct((hidden, half), f32),
+            jax.ShapeDtypeStruct((hidden, half), bf16),
         ),
-        in_specs=[vmem] * 8,
-        out_specs=(vmem, vmem),
+        in_specs=[here, vmem, vmem] + [here] * 5,
+        out_specs=(vmem, vmem, vmem),
         scratch_shapes=[
+            pltpu.VMEM(saved_gate.shape, bf16),
+            pltpu.VMEM(saved_up.shape, bf16),
+            pltpu.VMEM(w_gate.shape, bf16),
+            pltpu.VMEM(w_up.shape, bf16),
+            pltpu.VMEM(w_down.shape, bf16),
             pltpu.VMEM((blocks * tok, width), bf16),
             pltpu.VMEM((blocks, experts, 2 * tok), f32),
             pltpu.VMEM((hidden, blocks * tok), bf16),
             pltpu.VMEM((n_group, rows_g, hidden), f32),
             pltpu.VMEM((n_group, rows_g, hidden), f32),
-            pltpu.VMEM((n_group, rows_g, half), bf16),
+            pltpu.VMEM((n_group, rows_g, half), f32),
             pltpu.VMEM((n_group, rows_g, half), bf16),
             pltpu.VMEM((n_group, rows_g, half), bf16),
             pltpu.VMEM((n_group, 2, 2, tok, half), bf16),
@@ -481,25 +526,34 @@
             pltpu.VMEM((n_group, tok, half), bf16),
             pltpu.VMEM((n_group, tok, half), bf16),
             pltpu.VMEM((hidden, half), bf16),
-            pltpu.VMEM((hidden, half), bf16),
             pltpu.SemaphoreType.DMA((kinds, n_group)),
             pltpu.SemaphoreType.DMA((kinds, n_group)),
             pltpu.SemaphoreType.DMA((2,)),
-            pltpu.SemaphoreType.DMA,
+            pltpu.SemaphoreType.DMA((6,)),
         ],
         compiler_params=pltpu.CompilerParams(
-            collective_id=0, has_side_effects=True, vmem_limit_bytes=60 * 1024 * 1024
+            collective_id=0, has_side_effects=True, vmem_limit_bytes=40 * 1024 * 1024
         ),
     )(
         cotangent,
-        expert_ids[0],
-        gate_probs[0],
+        expert_ids[0].T,
+        gate_probs[0].T,
         saved_gate,
         saved_up,
         w_gate,
         w_up,
         w_down,
     )
+    return pl.pallas_call(
+        finish_kernel,
+        out_shape=(
+            jax.ShapeDtypeStruct((tok, half), bf16),
+            jax.ShapeDtypeStruct((1, hidden, half), f32),
+        ),
+        in_specs=[vmem] * 3,
+        out_specs=(vmem, vmem),
+        compiler_params=pltpu.CompilerParams(vmem_limit_bytes=8 * 1024 * 1024),
+    )(rows, own, other)
 
 
 def on_device(cotangent, expert_ids, gate_probs, saved_gate, saved_up, w_gate, w_up, w_down):

time: 68.9 us -> 60.4 us (0.88)
  local copies, waits for them, and re-layouts: 7.06 us -> 1.36 us
  Pallas kernels: 60.4 us -> 57.5 us
    unnamed x4, local copies, waits for them, and re-layouts: 7.06 us -> 1.36 us
    pallas_call x1, Pallas kernels: 60.4 us -> 56.1 us  [dense_plan(): pl.pallas_call(functools.partial(dense_kernel, n_group, n_expert), out_sh...]
    pallas_call x0 -> x1, Pallas kernels: none -> 1.32 us  [dense_plan(): pl.pallas_call(finish_kernel, out_shape=(jax.ShapeDtypeStruct((tok, half)...]
where the time goes in v2:
time: 60.4 us; the launch traced here: 59.5 us
  Pallas kernels  57.5 us (95%)
  local copies, waits for them, and re-layouts  1.36 us (2%)
  between operations  0.65 us (1%)
    pallas_call x1, Pallas kernels, dense_plan(): pl.pallas_call(functools.partial(dense_kernel, n_group, n_expert), out_sh...  56.1 us
    unnamed x4, local copies, waits for them, and re-layouts  1.36 us
    pallas_call x1, Pallas kernels, dense_plan(): pl.pallas_call(finish_kernel, out_shape=(jax.ShapeDtypeStruct((tok, half)...  1.32 us

profile of v2, /device:TPU:0, one launch (start us, length us, event | category | flops | bytes accessed | tf_op | source)
XLA Modules:
  0.0 59.5 jit_solution(16702597843162024916)
XLA Ops:
  0.6 0.0 copy-start
  0.6 0.7 %copy-done = s32[1,64,4]{1,2,0:T(4,128)S(1)} copy-done((s32[1,64,4]{1,2,0:T(4,128)S(1)}, s32[1,64,4]{1,2,0:T(4,128)}, u32[]{:S(2)}) %copy-start) | copy-done | bytes 1048
  1.3 0.0 copy-start.1
  1.3 0.7 %copy-done.1 = f32[1,64,4]{1,2,0:T(4,128)S(1)} copy-done((f32[1,64,4]{1,2,0:T(4,128)S(1)}, f32[1,64,4]{1,2,0:T(4,128)}, u32[]{:S(2)}) %copy-start.1) | copy-done | bytes 1048
  2.0 56.1 %shard_map.95 = (bf16[64,1024]{1,0:T(8,128)(2,1)S(1)}, f32[384,1024]{1,0:T(8,128)S(1)}, bf16[384,1024]{1,0:T(8,128)(2,1)S(1)}) custom-call(bf16[64,2048]{1,0:T(8,128)(2,1)} %cot_ref.1, s32[4,64]{1,0:T(4,128)S(1)} %bitcast.6, f32[4,64]{1,0:T(4,128)S(1)} %bitcast.7, bf16[1,1024,384]{2,1,0:T(8,128)(2,1)} %sg_hbm.1, bf16[1,1024,384]{2,1,0:T(8,128)(2,1)} %su_hbm.1, ...), custom_call_target="tpu_custom_call" | custom-call | tf_op jit(solution)/shard_map/pallas_call | solution.py:496
  58.1 1.3 %shard_map.96 = (bf16[64,1024]{1,0:T(8,128)(2,1)}, f32[1,384,1024]{2,1,0:T(8,128)}) custom-call(bf16[64,1024]{1,0:T(8,128)(2,1)S(1)} %get-tuple-element.5.rows_ref, f32[384,1024]{1,0:T(8,128)S(1)} %get-tuple-element.6.own_ref, bf16[384,1024]{1,0:T(8,128)(2,1)S(1)} %get-tuple-element.7.other_ref), custom_call_target="tpu_custom_call" | custom-call | tf_op jit(solution)/shard_map/pallas_call | solution.py:547
Async XLA Ops:
  0.6 0.7 %copy-start = (s32[1,64,4]{1,2,0:T(4,128)S(1)}, s32[1,64,4]{1,2,0:T(4,128)}, u32[]{:S(2)}) copy-start(s32[1,64,4]{1,2,0:T(4,128)} %param.9) | copy-start | bytes 3076
  1.3 0.7 %copy-start.1 = (f32[1,64,4]{1,2,0:T(4,128)S(1)}, f32[1,64,4]{1,2,0:T(4,128)}, u32[]{:S(2)}) copy-start(f32[1,64,4]{1,2,0:T(4,128)} %param.10) | copy-start | bytes 3076

commit v3 on v2

--- a/solution.py
+++ b/solution.py
@@ -346,7 +346,7 @@
     def compute(i):
         q = group_at(i)
 
-        @pl.when(i == 0)
+        @pl.when(i == 1)
         def _():
             for load in loads[2:]:
                 load.wait()
@@ -418,14 +418,15 @@
 
     stages = (ag_first, ag_second, ag_third, compute, rs_first, rs_second, rs_third)
     order = (0, 1, 4, 5, 6, 2, 3)
-    last = n_group + len(stages) - 1
+    lags = (0, 1, 2, 4, 5, 6, 7)
+    last = n_group + lags[-1]
 
     def step(s, carry):
-        for lag in order:
-
-            @pl.when((s >= lag) & (s < lag + n_group))
-            def _(lag=lag):
-                stages[lag](s - lag)
+        for k in order:
+
+            @pl.when((s >= lags[k]) & (s < lags[k] + n_group))
+            def _(k=k):
+                stages[k](s - lags[k] if k < 3 else (s - lags[k] + 1) % n_group)
 
         @pl.when(s >= last - 4)
         def _():
@@ -491,6 +492,10 @@
     cotangent, saved_gate, saved_up, w_gate, w_up, w_down = (
         pltpu.with_memory_space_constraint(value, pltpu.HBM)
         for value in (cotangent, saved_gate, saved_up, w_gate, w_up, w_down)
+    )
+    ids, probs = (
+        pltpu.with_memory_space_constraint(value[0].T, pltpu.HBM)
+        for value in (expert_ids, gate_probs)
     )
     here = pl.BlockSpec(memory_space=pltpu.HBM)
     rows, own, other = pl.pallas_call(
@@ -536,8 +541,8 @@
         ),
     )(
         cotangent,
-        expert_ids[0].T,
-        gate_probs[0].T,
+        ids,
+        probs,
         saved_gate,
         saved_up,
         w_gate,

time: 60.4 us -> 58.8 us (0.974); the launches traced: 59.5 us -> 58.6 us
  local copies, waits for them, and re-layouts: 1.36 us -> 0 us
    unnamed x4 -> x0, local copies, waits for them, and re-layouts: 1.36 us -> none
where the time goes in v3:
time: 58.8 us; the launch traced here: 58.6 us
  Pallas kernels  57.9 us (98%)
  between operations  0.64 us (1%)
    pallas_call x1, Pallas kernels, dense_plan(): pl.pallas_call(functools.partial(dense_kernel, n_group, n_expert), out_sh...  56.6 us
    pallas_call x1, Pallas kernels, dense_plan(): pl.pallas_call(finish_kernel, out_shape=(jax.ShapeDtypeStruct((tok, half)...  1.32 us

profile of v3, /device:TPU:0, one launch (start us, length us, event | category | flops | bytes accessed | tf_op | source)
XLA Modules:
  0.0 58.6 jit_solution(12097610238018355622)
XLA Ops:
  0.6 56.6 %shard_map.95 = (bf16[64,1024]{1,0:T(8,128)(2,1)S(1)}, f32[384,1024]{1,0:T(8,128)S(1)}, bf16[384,1024]{1,0:T(8,128)(2,1)S(1)}) custom-call(bf16[64,2048]{1,0:T(8,128)(2,1)} %cot_ref.1, s32[4,64]{1,0:T(4,128)} %bitcast.6, f32[4,64]{1,0:T(4,128)} %bitcast.7, bf16[1,1024,384]{2,1,0:T(8,128)(2,1)} %sg_hbm.1, bf16[1,1024,384]{2,1,0:T(8,128)(2,1)} %su_hbm.1, ...), custom_call_target="tpu_custom_call" | custom-call | tf_op jit(solution)/shard_map/pallas_call | solution.py:501
  57.3 1.3 %shard_map.96 = (bf16[64,1024]{1,0:T(8,128)(2,1)}, f32[1,384,1024]{2,1,0:T(8,128)}) custom-call(bf16[64,1024]{1,0:T(8,128)(2,1)S(1)} %get-tuple-element.5.rows_ref, f32[384,1024]{1,0:T(8,128)S(1)} %get-tuple-element.6.own_ref, bf16[384,1024]{1,0:T(8,128)(2,1)S(1)} %get-tuple-element.7.other_ref), custom_call_target="tpu_custom_call" | custom-call | tf_op jit(solution)/shard_map/pallas_call | solution.py:552
